TPU v7x, 128 devices: a whole 4x4x4 slice. The times are simulated.
128 devices in a mesh: tm: 16 (over y, x), orb: 8 (over z, core).
Axes of the slice: x: 4, y: 4, z: 4, core: 2. Of those that a mesh axis runs over, the one named last changes fastest.
Arguments:
- forward: bfloat16 [2, 2, 512, 128, 128], P(None, None, 'tm'), may hold values from -2 to 2
- backward_slab: bfloat16 [2, 2, 512, 128, 128], P(None, None, 'tm', 'orb'), may hold values from -2 to 2
- slot_time: int32 [512], replicated, may hold values from 0 to 511, as said below
- pattern: int32 [128, 128], replicated, may hold values 0 or 1
- coupling: float32 [128, 128], replicated, may hold values from -1 to 1
- hamiltonian: float32 [128, 128], replicated, may hold values from -0.8 to 0.8
- lesser_now: float32 [2, 128, 128], replicated, may hold values from -1.5 to 1.5
Outputs:
- lesser_next: float32 [2, 128, 128], P(None, 'orb')
Inputs may be any that keep to these rules, and one draw needn't show every extreme that they name: slot_time is a permutation of the 512 history times. The 32 slots of each index d of tm hold exactly 32 // 16 times of the range [e * 32, (e + 1) * 32) for every index e of tm.
All inputs are finite; a program needn't handle non-finite values.
Results may differ from a plain program's by a relative error of at most 0.0054.
Values may be sent and summed in bfloat16 or wider, within the bound.
No kernel may reach another device: no remote copies, remote signals or barrier semaphores. Data moves between devices by JAX's collectives and lax.ppermute only.
A program may use at most 64 MiB of HBM per device.

v0:
```python
import math

import jax
import jax.numpy as jnp
from jax import lax
from jax.sharding import PartitionSpec as P

history_step = 0.02
update_step = 0.5


def complex_einsum(form, left_re, left_im, right_re, right_im):
    real_part = jnp.einsum(
        form, left_re, right_re, preferred_element_type=jnp.float32
    ) - jnp.einsum(form, left_im, right_im, preferred_element_type=jnp.float32)
    imag_part = jnp.einsum(
        form, left_re, right_im, preferred_element_type=jnp.float32
    ) + jnp.einsum(form, left_im, right_re, preferred_element_type=jnp.float32)
    return (real_part, imag_part)


def self_energy(fwd_re, fwd_im, back_re, back_im, interaction, inter_rows, row_start, row_count):
    rows_re = lax.dynamic_slice_in_dim(fwd_re, row_start, row_count, 1)
    rows_im = lax.dynamic_slice_in_dim(fwd_im, row_start, row_count, 1)
    fwd_re32 = fwd_re.astype(jnp.float32)
    fwd_im32 = fwd_im.astype(jnp.float32)
    trans_re = jnp.swapaxes(back_re, 1, 2).astype(jnp.float32)
    trans_im = jnp.swapaxes(back_im, 1, 2).astype(jnp.float32)
    bubble_re = (fwd_re32 * trans_re - fwd_im32 * trans_im).astype(jnp.bfloat16)
    bubble_im = (fwd_re32 * trans_im + fwd_im32 * trans_re).astype(jnp.bfloat16)
    left_re = jnp.einsum(
        "ik,skj->sij", inter_rows, bubble_re, preferred_element_type=jnp.float32
    ).astype(jnp.bfloat16)
    left_im = jnp.einsum(
        "ik,skj->sij", inter_rows, bubble_im, preferred_element_type=jnp.float32
    ).astype(jnp.bfloat16)
    screen_re = jnp.einsum("sik,kj->sij", left_re, interaction, preferred_element_type=jnp.float32)
    screen_im = jnp.einsum("sik,kj->sij", left_im, interaction, preferred_element_type=jnp.float32)
    rows_re32 = rows_re.astype(jnp.float32)
    rows_im32 = rows_im.astype(jnp.float32)
    direct_re = rows_re32 * screen_re - rows_im32 * screen_im
    direct_im = rows_re32 * screen_im + rows_im32 * screen_re
    inter_rows32 = inter_rows.astype(jnp.float32)
    scaled_re = (inter_rows32[None, :, :, None] * fwd_re32[:, None]).astype(jnp.bfloat16)
    scaled_im = (inter_rows32[None, :, :, None] * fwd_im32[:, None]).astype(jnp.bfloat16)
    inner_re, inner_im = complex_einsum("slm,simj->silj", back_re, back_im, scaled_re, scaled_im)
    inter32 = interaction.astype(jnp.float32)
    weighted_re = (inner_re * inter32).astype(jnp.bfloat16)
    weighted_im = (inner_im * inter32).astype(jnp.bfloat16)
    exch_re, exch_im = complex_einsum("sil,silj->sij", rows_re, rows_im, weighted_re, weighted_im)
    sigma_re = (direct_re - exch_re).astype(jnp.bfloat16)
    sigma_im = (direct_im - exch_im).astype(jnp.bfloat16)
    return (sigma_re, sigma_im)


def block_terms(fwd_block, back_block, weights, interaction, inter_rows, row_start, row_count):
    summed = None
    scale = weights[:, None, None]
    for branch in (0, 1):
        other = 1 - branch
        factor = 1.0 if branch == 0 else -1.0
        sigma_re, sigma_im = self_energy(
            fwd_block[branch, 0],
            fwd_block[branch, 1],
            back_block[other, 0],
            back_block[other, 1],
            interaction,
            inter_rows,
            row_start,
            row_count,
        )
        prod_re, prod_im = complex_einsum(
            "sil,slj->sij", sigma_re, sigma_im, back_block[other, 0], back_block[other, 1]
        )
        term = factor * jnp.stack(
            [jnp.sum(scale * prod_re, axis=0), jnp.sum(scale * prod_im, axis=0)]
        )
        summed = term if summed is None else summed + term
    return summed


def history_terms(fwd_part, back_part, weights, interaction, inter_rows, row_start, row_count):
    slices_here = fwd_part.shape[2]
    block_size = math.gcd(max(4, 128 // row_count), slices_here)
    block_count = slices_here // block_size
    orbitals = fwd_part.shape[3]

    def add_block(block, running):
        start = block * block_size
        fwd_block = lax.dynamic_slice_in_dim(fwd_part, start, block_size, 2)
        back_block = lax.dynamic_slice_in_dim(back_part, start, block_size, 2)
        weight_block = lax.dynamic_slice_in_dim(weights, start, block_size, 0)
        return running + block_terms(
            fwd_block, back_block, weight_block, interaction, inter_rows, row_start, row_count
        )

    initial = jnp.zeros((2, row_count, orbitals), jnp.float32)
    return lax.fori_loop(0, block_count, add_block, initial)


def on_device(forward, backward_slab, slot_time, pattern, coupling, hamiltonian, lesser_now):
    tm_count = lax.axis_size("tm")
    my_time = lax.axis_index("tm")
    my_orb = lax.axis_index("orb")
    per_device = forward.shape[2]
    row_count = backward_slab.shape[3]
    per_peer = per_device // tm_count
    slices_all = per_device * tm_count
    row_start = my_orb * row_count
    time_start = my_time * per_device
    holder_of = slot_time // per_device
    my_holders = lax.dynamic_slice_in_dim(holder_of, time_start, per_device)
    send_order = jnp.argsort(my_holders, stable=True)
    sorted_slab = jnp.take(backward_slab, send_order, axis=2)
    holder_grid = holder_of.reshape(tm_count, per_device)
    time_grid = slot_time.reshape(tm_count, per_device)
    not_mine = (holder_grid != my_time).astype(jnp.int32)
    positions = jnp.argsort(not_mine, axis=1, stable=True)[:, :per_peer]
    times_here = jnp.take_along_axis(time_grid, positions, axis=1).reshape(per_device)
    natural = jnp.argsort(times_here - time_start)
    masked = coupling * pattern.astype(jnp.float32)
    interaction = ((masked + masked.T) * 0.5).astype(jnp.bfloat16)
    inter_rows = lax.dynamic_slice_in_dim(interaction, row_start, row_count, 0)
    time_index = time_start + jnp.arange(per_device, dtype=jnp.int32)
    edges = (time_index == 0) | (time_index == slices_all - 1)
    weights = jnp.where(edges, jnp.float32(0.5), jnp.float32(1.0)) * history_step
    full_sorted = lax.all_gather(sorted_slab, "orb", axis=3, tiled=True)
    arrived = lax.all_to_all(full_sorted, "tm", split_axis=2, concat_axis=2, tiled=True)
    back_full = jnp.take(arrived, natural, axis=2)
    local_collision = history_terms(
        forward, back_full, weights, interaction, inter_rows, row_start, row_count
    )
    summed_rows = lax.psum(local_collision, "tm")
    collision = lax.all_gather(summed_rows, "orb", axis=1, tiled=True)
    own_rows = lax.dynamic_slice_in_dim(collision, row_start, row_count, 1)
    own_columns = lax.dynamic_slice_in_dim(collision, row_start, row_count, 2)
    herm_re = own_rows[0] + own_columns[0].T
    herm_im = own_rows[1] - own_columns[1].T
    high = lax.Precision.HIGHEST
    ham_rows = lax.dynamic_slice_in_dim(hamiltonian, row_start, row_count, 0)
    lesser_rows = lax.dynamic_slice_in_dim(lesser_now, row_start, row_count, 1)
    comm_re = jnp.dot(ham_rows, lesser_now[0], precision=high) - jnp.dot(
        lesser_rows[0], hamiltonian, precision=high
    )
    comm_im = jnp.dot(ham_rows, lesser_now[1], precision=high) - jnp.dot(
        lesser_rows[1], hamiltonian, precision=high
    )
    next_re = lesser_rows[0] + update_step * (comm_im + herm_im)
    next_im = lesser_rows[1] - update_step * (comm_re + herm_re)
    return jnp.stack([next_re, next_im])


def solution(mesh):
    in_specs = (
        P(None, None, "tm", None, None),
        P(None, None, "tm", "orb", None),
        P(),
        P(),
        P(),
        P(),
        P(),
    )
    out_specs = P(None, "orb", None)
    return jax.shard_map(
        on_device, mesh=mesh, in_specs=in_specs, out_specs=out_specs, check_vma=False
    )
```

profile of v0, /device:TPU:1, one launch (start us, length us, event | category | flops | bytes accessed | tf_op | source)
XLA Modules:
  0.0 479.1 jit_solution(11907473625283810762)
XLA Ops:
  10.6 39.5 %all-gather.2.cloned.1.call-done = bf16[2,2,32,128,128]{4,3,1,0,2:T(8,128)(2,1)} async-done(((bf16[2,2,32,16,128]{4,3,1,0,2:T(8,128)(2,1)}), bf16[2,2,32,128,128]{4,3,1,0,2:T(8,128)(2,1)}) %all-gather.2.cloned.1.call-update) | async-done | bytes 4194320 | tf_op jit(solution)/shard_map/all_gather | solution.py:127
  50.1 6.6 %all-to-all-start = ((bf16[2,2,32,128,128]{4,3,1,0,2:T(8,128)(2,1)}), bf16[2,2,32,128,128]{4,3,1,0,2:T(8,128)(2,1)}, u32[]{:S(2)}, u32[]{:S(2)}) async-start(bf16[2,2,32,128,128]{4,3,1,0,2:T(8,128)(2,1)} %all-gather.2.cloned.1.call-done), calls=%async_computation | async-start | bytes 8388608 | tf_op jit(solution)/shard_map/all_to_all | solution.py:128
  64.0 55.6 %all-to-all-done = bf16[2,2,32,128,128]{4,3,1,0,2:T(8,128)(2,1)} async-done(((bf16[2,2,32,128,128]{4,3,1,0,2:T(8,128)(2,1)}), bf16[2,2,32,128,128]{4,3,1,0,2:T(8,128)(2,1)}, u32[]{:S(2)}, u32[]{:S(2)}) %all-to-all-start) | async-done | bytes 4194336 | tf_op jit(solution)/shard_map/all_to_all | solution.py:128
  119.6 4.7 copy.45
  124.3 5.2 %gather_fusion.1 = bf16[32,2,2,128,128]{4,3,2,1,0:T(8,128)(2,1)} fusion(bf16[2,2,32,128,128]{4,3,2,1,0:T(8,128)(2,1)} %copy.45, s32[1024]{0:T(1024)S(1)} %pad_clamp_fusion), kind=kCustom, calls=%fused_computation.1 | custom fusion | bytes 8388736 | tf_op jit(solution)/shard_map/jit(_take)/gather | solution.py:129
  129.5 4.6 select_bitcast_fusion
  134.1 249.0 %while.16 = (s32[]{:T(128)}, f32[2,16,128]{2,1,0:T(8,128)}, f32[32]{0:T(128)S(1)}, bf16[2,2,32,128,128]{4,3,2,1,0:T(8,128)(2,1)}, s32[]{:T(128)}, /*index=5*/bf1...) while((s32[]{:T(128)}, f32[2,16,128]{2,1,0:T(8,128)}, ...), condition=%wide.region_8.9_spmd.clone, body=%wide.region_3.8_spmd.clone.sunk | while | flops 4459808768 | bytes 142112496 | solution.py:98
  148.4 2.6 fusion.413
  157.8 2.6 fusion.410
  173.2 2.6 fusion.427
  182.6 2.6 fusion.424
  210.6 2.6 fusion.413
  220.0 2.6 fusion.410
  235.4 2.6 fusion.427
  244.8 2.6 fusion.424
  272.9 2.6 fusion.413
  282.3 2.6 fusion.410
  297.6 2.6 fusion.427
  307.0 2.6 fusion.424
  335.1 2.6 fusion.413
  344.5 2.6 fusion.410
  359.9 2.6 fusion.427
  383.1 58.1 %psum.7 = f32[2,16,128]{2,1,0:T(8,128)S(1)} all-reduce(f32[2,16,128]{2,1,0:T(8,128)} %get-tuple-element.204), channel_id=1, replica_groups=mesh['tm'=16,'orb'=8] {'tm'}, use_global_device_ids=true, to_apply=%region_9.10 | all-reduce | flops 4096 | bytes 32768 | tf_op jit(solution)/shard_map/psum | solution.py:133
  441.1 28.1 %all_gather.7 = f32[2,128,128]{2,1,0:T(8,128)S(1)} all-gather(f32[2,16,128]{2,1,0:T(8,128)S(1)} %psum.7), channel_id=1, replica_groups=mesh['tm'=16,'orb'=8] {'orb'}, dimensions={1}, use_global_device_ids=true | all-gather | bytes 147456 | tf_op jit(solution)/shard_map/all_gather | solution.py:134
  (295 shorter events, 222.7 us)
Async XLA Ops:
  6.5 43.6 %all-gather.2.cloned.1.call-start = ((), (), s32[]{:S(2)}) async-start(), calls=%async_computation.1 | async-start | bytes 4718592 | tf_op jit(solution)/shard_map/all_gather | solution.py:127
  10.6 46.1 %copy-start.11 = (s32[512]{0:T(512)S(1)}, s32[512]{0:T(512)}, u32[]{:S(2)}) copy-start(s32[512]{0:T(512)} %param.11) | copy-start | bytes 6148
  50.1 69.5 %all-to-all-start = ((bf16[2,2,32,128,128]{4,3,1,0,2:T(8,128)(2,1)}), bf16[2,2,32,128,128]{4,3,1,0,2:T(8,128)(2,1)}, u32[]{:S(2)}, u32[]{:S(2)}) async-start(bf16[2,2,32,128,128]{4,3,1,0,2:T(8,128)(2,1)} %all-gather.2.cloned.1.call-done), calls=%async_computation | async-start | bytes 8388608 | tf_op jit(solution)/shard_map/all_to_all | solution.py:128
  134.1 6.7 %copy-start.2 = (bf16[128,128]{1,0:T(8,128)(2,1)}, bf16[128,128]{1,0:T(8,128)(2,1)S(1)}, u32[]{:S(2)}) copy-start(bf16[128,128]{1,0:T(8,128)(2,1)S(1)} %get-tuple-element.394) | copy-start | bytes 98308 | tf_op jit(solution)/shard_map/while
  185.2 4.5 copy-start.3
  185.2 4.5 copy-start.4
  187.5 8.3 %copy-start.6 = (f32[2,16,128]{2,1,0:T(8,128)S(1)}, f32[2,16,128]{2,1,0:T(8,128)}, u32[]{:S(2)}) copy-start(f32[2,16,128]{2,1,0:T(8,128)} %get-tuple-element.375) | copy-start | bytes 49156 | tf_op jit(solution)/shard_map/while
  187.5 8.9 %copy-start.13 = (f32[32]{0:T(128)S(1)}, f32[32]{0:T(128)}, u32[]{:S(2)}) copy-start(f32[32]{0:T(128)} %copy-done.12) | copy-start | bytes 388 | tf_op jit(solution)/shard_map/while
  196.4 6.7 %copy-start.2 = (bf16[128,128]{1,0:T(8,128)(2,1)}, bf16[128,128]{1,0:T(8,128)(2,1)S(1)}, u32[]{:S(2)}) copy-start(bf16[128,128]{1,0:T(8,128)(2,1)S(1)} %get-tuple-element.394) | copy-start | bytes 98308 | tf_op jit(solution)/shard_map/while
  247.4 4.5 copy-start.3
  247.4 4.5 copy-start.4
  249.7 8.3 %copy-start.6 = (f32[2,16,128]{2,1,0:T(8,128)S(1)}, f32[2,16,128]{2,1,0:T(8,128)}, u32[]{:S(2)}) copy-start(f32[2,16,128]{2,1,0:T(8,128)} %get-tuple-element.375) | copy-start | bytes 49156 | tf_op jit(solution)/shard_map/while
  249.7 8.9 %copy-start.13 = (f32[32]{0:T(128)S(1)}, f32[32]{0:T(128)}, u32[]{:S(2)}) copy-start(f32[32]{0:T(128)} %copy-done.12) | copy-start | bytes 388 | tf_op jit(solution)/shard_map/while
  258.6 6.7 %copy-start.2 = (bf16[128,128]{1,0:T(8,128)(2,1)}, bf16[128,128]{1,0:T(8,128)(2,1)S(1)}, u32[]{:S(2)}) copy-start(bf16[128,128]{1,0:T(8,128)(2,1)S(1)} %get-tuple-element.394) | copy-start | bytes 98308 | tf_op jit(solution)/shard_map/while
  309.7 4.5 copy-start.3
  309.7 4.5 copy-start.4
  311.9 8.3 %copy-start.6 = (f32[2,16,128]{2,1,0:T(8,128)S(1)}, f32[2,16,128]{2,1,0:T(8,128)}, u32[]{:S(2)}) copy-start(f32[2,16,128]{2,1,0:T(8,128)} %get-tuple-element.375) | copy-start | bytes 49156 | tf_op jit(solution)/shard_map/while
  311.9 8.9 %copy-start.13 = (f32[32]{0:T(128)S(1)}, f32[32]{0:T(128)}, u32[]{:S(2)}) copy-start(f32[32]{0:T(128)} %copy-done.12) | copy-start | bytes 388 | tf_op jit(solution)/shard_map/while
  320.8 6.7 %copy-start.2 = (bf16[128,128]{1,0:T(8,128)(2,1)}, bf16[128,128]{1,0:T(8,128)(2,1)S(1)}, u32[]{:S(2)}) copy-start(bf16[128,128]{1,0:T(8,128)(2,1)S(1)} %get-tuple-element.394) | copy-start | bytes 98308 | tf_op jit(solution)/shard_map/while
  371.9 4.5 copy-start.3
  371.9 4.5 copy-start.4
  374.2 8.3 %copy-start.6 = (f32[2,16,128]{2,1,0:T(8,128)S(1)}, f32[2,16,128]{2,1,0:T(8,128)}, u32[]{:S(2)}) copy-start(f32[2,16,128]{2,1,0:T(8,128)} %get-tuple-element.375) | copy-start | bytes 49156 | tf_op jit(solution)/shard_map/while
  374.2 8.9 %copy-start.13 = (f32[32]{0:T(128)S(1)}, f32[32]{0:T(128)}, u32[]{:S(2)}) copy-start(f32[32]{0:T(128)} %copy-done.12) | copy-start | bytes 388 | tf_op jit(solution)/shard_map/while
  383.1 89.1 %copy-start.1 = (bf16[2,2,32,16,128]{4,3,2,1,0:T(8,128)(2,1)S(1)}, bf16[2,2,32,16,128]{4,3,2,1,0:T(8,128)(2,1)}, u32[]{:S(2)}) copy-start(bf16[2,2,32,16,128]{4,3,2,1,0:T(8,128)(2,1)} %param.10) | copy-start | bytes 1572868
  (16 other events, 30.4 us)
Sparse Core Ops, SparseCore 0:
  10.7 39.3 all-gather.1
where the time goes:
time: 482 us; the launch traced here: 479 us
  matrix products  219 us (45%)
  waiting for transfers between devices  95.1 us (20%)
  blocking collectives  86.2 us (18%)
  local copies, waits for them, and re-layouts  46.3 us (10%)
  between operations  13.6 us (3%)
  other arithmetic  11.6 us (2%)
  starting transfers between devices  6.58 us (1%)
    psum x1, blocking collectives, on_device(): summed_rows = lax.psum(local_collision, 'tm')  58.1 us
    all_to_all x1, waiting for transfers between devices, on_device(): lax.all_to_all(full_sorted, 'tm', split_axis=2, concat_axis=2, tiled=True)  55.6 us
    dot_general x24, matrix products, complex_einsum(): jnp.einsum(form, left_re, right_im, preferred_element_type=jnp.float32)  48.3 us
    dot_general x24, matrix products, complex_einsum(): jnp.einsum(form, left_im, right_im, preferred_element_type=jnp.float32)  48.2 us
    dot_general x24, matrix products, complex_einsum(): jnp.einsum(form, left_im, right_re, preferred_element_type=jnp.float32)  45 us
    dot_general x24, matrix products, complex_einsum(): jnp.einsum(form, left_re, right_re, preferred_element_type=jnp.float32)  44.8 us
    all_gather x1, waiting for transfers between devices, on_device(): full_sorted = lax.all_gather(sorted_slab, 'orb', axis=3, tiled=True)  39.5 us
    all_gather x1, blocking collectives, on_device(): collision = lax.all_gather(summed_rows, 'orb', axis=1, tiled=True)  28.1 us
  transfers between devices with their start and end apart: 2, of which 2 were waited for; matrix products, arithmetic and copies ran while one was open for 1% of the time, Pallas kernels for 0%

commit v1 on v0

v1 whole, which is shorter than its diff:
```python
import jax
import jax.numpy as jnp
from jax import lax
from jax.experimental import pallas as pl
from jax.experimental.pallas import tpu as pltpu
from jax.sharding import PartitionSpec as P

N = 128
bf = jnp.bfloat16
f32 = jnp.float32
HISTORY_STEP = 0.02
UPDATE_STEP = 0.5
UNITS = [(kk, a) for kk in range(4) for a in range(2)]


def rows16(row):
    return jnp.broadcast_to(row, (16, N)).astype(bf)


def cat0(parts):
    return jnp.concatenate(parts, axis=0)


def cat1(parts):
    return jnp.concatenate(parts, axis=1)


def collide(wts, f0, f1, brecv, coup, patt, out, vb, vv, ft, bt, dirt, sig):
    masked = coup[...] * patt[...].astype(f32)
    inter = ((masked + masked.T) * 0.5).astype(bf)
    vv[...] = inter.astype(f32)
    for m in range(N):
        vb[m] = jnp.broadcast_to(vv[:, m:m + 1], (N, N))

    def fmat(kk, a, c):
        return (f0, f1)[kk // 2][kk % 2, a, c]

    def bmat(kk, a, c):
        return cat0([brecv[o, 1 - a, c, kk] for o in range(8)])

    def direct(*accs):
        zero = jnp.zeros((N, N), bf)
        wide = jnp.zeros((N, 2 * N), bf)
        for u, (kk, a) in enumerate(UNITS):
            fr = fmat(kk, a, 0).astype(f32)
            fi = fmat(kk, a, 1).astype(f32)
            tr = bmat(kk, a, 0).T.astype(f32)
            ti = bmat(kk, a, 1).T.astype(f32)
            ft[u, 0] = fr
            ft[u, 1] = fi
            bt[u, 0] = tr
            bt[u, 1] = ti
            bub = cat1([(fr * tr - fi * ti).astype(bf), (fr * ti + fi * tr).astype(bf)])
            stage = (u // 2) % 2
            pltpu.matmul_push_rhs(cat0([bub, wide]), stage, u % 2)
            pltpu.matmul_acc_lhs(accs[u], cat1([inter, zero]), load_staged_rhs=stage)
        both = cat0([cat1([inter, zero]), cat1([zero, inter])])
        for x in range(2):
            pltpu.matmul_push_rhs(both, 0, x)
        lefts = [pltpu.matmul_pop(accs[u]).astype(bf) for u in range(8)]
        for u in range(8):
            pltpu.matmul_acc_lhs(accs[u], lefts[u], load_staged_rhs=0 if u < 2 else None)
        for u in range(8):
            scr = pltpu.matmul_pop(accs[u])
            fr, fi = ft[u, 0], ft[u, 1]
            sr, si = scr[:, :N], scr[:, N:]
            dirt[u, :, :N] = fr * sr - fi * si
            dirt[u, :, N:] = fr * si + fi * sr

    pl.run_scoped(direct, *[pltpu.ACC(u % 2)((N, 2 * N), f32) for u in range(8)])

    def weights(u, m):
        half = []
        for x in range(2):
            fvr = rows16(ft[u, 0, pl.ds(m + x, 1), :])
            fvi = rows16(ft[u, 1, pl.ds(m + x, 1), :])
            v = [vv[16 * i:16 * i + 16].astype(bf) for i in range(8)]
            half.append(cat1([cat0([w * fvr for w in v]), cat0([w * fvi for w in v])]))
        return cat0(half)

    def lhs_rows(u, m):
        re, im = [], []
        for x in range(2):
            bvr = rows16(bt[u, 0, pl.ds(m + x, 1), :])
            bvi = rows16(bt[u, 1, pl.ds(m + x, 1), :])
            pr, pi = [], []
            for i in range(8):
                sl = slice(16 * i, 16 * i + 16)
                a = ft[u, 0, sl].astype(bf)
                b = ft[u, 1, sl].astype(bf)
                v = vb[m + x, sl].astype(bf)
                pr.append((a * bvr - b * bvi) * v)
                pi.append((a * bvi + b * bvr) * v)
            re.append(cat0(pr))
            im.append(cat0(pi))
        return cat1(re), cat1(im)

    def exchange(*flat):
        def acc(u, x, c):
            return flat[4 * (u % 2) + 2 * x + c]

        def step(u, t, last=False):
            for q in range(2):
                base = 8 * t + 4 * q
                lhs = [lhs_rows(u, base + 2 * x) for x in range(2)]
                for x in range(2):
                    pltpu.matmul_acc_lhs(acc(u, x, 0), lhs[x][0], load_staged_rhs=q)
                if not (last and q):
                    for x in range(2):
                        pltpu.matmul_push_rhs(weights(u, base + 4 + 2 * x), 1 - q, x)
                elif u < 7:
                    for x in range(2):
                        pltpu.matmul_push_rhs(weights(u + 1, 2 * x), 0, x)
                for x in range(2):
                    pltpu.matmul_acc_lhs(acc(u, x, 1), lhs[x][1])

        def finish(u):
            rp = pltpu.matmul_pop(acc(u, 0, 0)) + pltpu.matmul_pop(acc(u, 1, 0))
            rq = pltpu.matmul_pop(acc(u, 0, 1)) + pltpu.matmul_pop(acc(u, 1, 1))
            sig[u, :, :N] = (dirt[u, :, :N] - (rp[:, :N] - rq[:, N:])).astype(bf)
            sig[u, :, N:] = (dirt[u, :, N:] - (rp[:, N:] + rq[:, :N])).astype(bf)

        for x in range(2):
            pltpu.matmul_push_rhs(weights(0, 2 * x), 0, x)
        for u in range(8):
            step(u, 0)
            if u:
                finish(u - 1)

            def loop(t, carry):
                step(u, t)
                return carry

            lax.fori_loop(1, N // 8 - 1, loop, 0)
            step(u, N // 8 - 1, True)
        finish(7)

    pl.run_scoped(exchange, *[pltpu.ACC(x)((N, 2 * N), f32) for x in (0, 0, 1, 1, 0, 0, 1, 1)])

    def product(*accs):
        for u, (kk, a) in enumerate(UNITS):
            br = bmat(kk, a, 0)
            bi = bmat(kk, a, 1)
            if a:
                br, bi = -br, -bi
            pltpu.matmul_push_rhs(cat0([cat1([br, bi]), cat1([-bi, br])]), a, kk % 2)
            pltpu.matmul_acc_lhs(accs[kk], sig[u], load_staged_rhs=a)
        total = wts[0] * pltpu.matmul_pop(accs[0])
        for kk in range(1, 4):
            total += wts[kk] * pltpu.matmul_pop(accs[kk])
        re = total[:, :N]
        im = total[:, N:]
        back_re = -0.5 * (re + re.T)
        back_im = 0.5 * (im - im.T)
        for o in range(8):
            out[o, 0] = back_im[16 * o:16 * o + 16]
            out[o, 1] = back_re[16 * o:16 * o + 16]

    pl.run_scoped(product, *[pltpu.ACC(kk % 2)((N, 2 * N), f32) for kk in range(4)])


def shift(orb, half):
    down = 2 * (orb % 2) + half
    return down, (down + orb // 2) % 4


def pack(times, fwd, slab, bsend, f0, f1, wts, seen, sems):
    me = lax.axis_index("tm")
    orb = lax.axis_index("orb")
    down = me // 4
    right = me % 4
    copies = []
    for half, dst in enumerate((f0, f1)):
        dy, dx = shift(orb, half)
        row = (((down + dy) % 4) * 4 + (right + dx) % 4) * 32

        def send(slot, found, dst=dst, half=half, row=row):
            when = times[row + slot]
            mine = when // 32 == me

            @pl.when(mine)
            def _():
                pltpu.make_async_copy(fwd.at[:, :, when % 32], dst.at[found], sems.at[2 * half + found]).start()

            return found + mine.astype(jnp.int32)

        lax.fori_loop(0, 32, send, 0)
        copies += [pltpu.make_async_copy(fwd.at[:, :, 0], dst.at[r], sems.at[2 * half + r]) for r in range(2)]
    for e in range(16):
        seen[e] = 0

    def place(slot, carry):
        when = times[me * 32 + slot]
        holder = when // 32
        rank = seen[holder]
        seen[holder] = rank + 1
        dy = (down - holder // 4 + 4) % 4
        dx = (right - holder % 4 + 4) % 4
        to = ((dx - dy + 4) % 4) * 2 + dy // 2
        spot = (dy % 2) * 2 + rank
        for a in range(2):
            for c in range(2):
                bsend[to, a, c, spot] = slab[a, c, slot]

        @pl.when(to == orb)
        def _():
            edge = jnp.logical_or(when == 0, when == 511)
            wts[spot] = jnp.where(edge, jnp.float32(0.5), jnp.float32(1.0)) * jnp.float32(HISTORY_STEP)

        return carry

    lax.fori_loop(0, 32, place, 0)
    for copy in copies:
        copy.wait()


def on_device(forward, backward_slab, slot_time, pattern, coupling, hamiltonian, lesser_now):
    smem = pl.BlockSpec(memory_space=pltpu.SMEM)
    vmem = pl.BlockSpec(memory_space=pltpu.VMEM)
    shape = jax.ShapeDtypeStruct
    bsend, f0, f1, wts = pl.pallas_call(
        pack,
        out_shape=(shape((8, 2, 2, 4, 16, N), bf), shape((2, 2, 2, N, N), bf), shape((2, 2, 2, N, N), bf),
                   shape((4,), f32)),
        in_specs=[smem, pl.BlockSpec(memory_space=pl.ANY), vmem],
        out_specs=(vmem, vmem, vmem, smem),
        scratch_shapes=[pltpu.SMEM((16,), jnp.int32), pltpu.SemaphoreType.DMA((4,))],
    )(slot_time, forward, backward_slab)
    moved = []
    for half, sent in enumerate((f0, f1)):
        pairs = []
        for e in range(16):
            for o in range(8):
                dy, dx = shift(o, half)
                d = ((e // 4 + dy) % 4) * 4 + (e % 4 + dx) % 4
                pairs.append((e * 8 + o, d * 8 + o))
        moved.append(lax.ppermute(sent, ("tm", "orb"), pairs))
    brecv = lax.all_to_all(bsend, "orb", 0, 0, tiled=True)
    V = pltpu.VMEM
    part = pl.pallas_call(
        collide,
        out_shape=shape((8, 2, 16, N), f32),
        in_specs=[smem] + [vmem] * 5,
        out_specs=vmem,
        scratch_shapes=[V((N, N, N), f32), V((N, N), f32), V((8, 2, N, N), f32), V((8, 2, N, N), f32),
                        V((8, N, 2 * N), f32), V((8, N, 2 * N), bf)],
    )(wts, moved[0], moved[1], brecv, coupling, pattern)
    own = lax.all_to_all(part, "orb", 0, 0, tiled=True).sum(0)
    spread = lax.all_to_all(jnp.broadcast_to(own[None], (16,) + own.shape), "tm", 0, 0, tiled=True)
    start = lax.axis_index("orb") * 16
    high = lax.Precision.HIGHEST
    ham_rows = lax.dynamic_slice_in_dim(hamiltonian, start, 16, 0)
    rows = lax.dynamic_slice_in_dim(lesser_now, start, 16, 1)
    ahead = jnp.dot(ham_rows, jnp.concatenate([lesser_now[0], lesser_now[1]], axis=1), precision=high)
    behind = jnp.dot(rows.reshape(32, N), hamiltonian, precision=high)
    comm_re = ahead[:, :N] - behind[:16]
    comm_im = ahead[:, N:] - behind[16:]
    base = rows + UPDATE_STEP * jnp.stack([comm_im, -comm_re])
    return base + spread.sum(0)


def solution(mesh):
    in_specs = (
        P(None, None, "tm", None, None),
        P(None, None, "tm", "orb", None),
        P(),
        P(),
        P(),
        P(),
        P(),
    )
    run = jax.shard_map(on_device, mesh=mesh, in_specs=in_specs, out_specs=P(None, "orb", None), check_vma=False)
    return run
```

time: 482 us -> 75.4 us (0.16)
  matrix products: 219 us -> 0.31 us
  blocking collectives: 86.2 us -> 0 us
  waiting for transfers between devices: 95.1 us -> 19.5 us
  local copies, waits for them, and re-layouts: 46.3 us -> 1.63 us
  Pallas kernels: 0 us -> 28.1 us
  starting transfers between devices: 6.58 us -> 23.8 us
  between operations: 13.6 us -> 0.07 us
  other arithmetic: 11.6 us -> 0.66 us
    dot_general x116 -> x2, matrix products: 219 us -> 0.31 us  [the longest x1 0.16 us: on_device(): jnp.dot(ham_rows, jnp.concatenate([lesser_now[0], lesser_now[1]], axis=1)...]
    psum x1 -> x0, blocking collectives: 58.1 us -> none  [on_device(): summed_rows = lax.psum(local_collision, 'tm')]
    all_to_all x1 -> x3, waiting for transfers between devices: 55.6 us -> 12.5 us  [the longest x1 7.4 us: on_device(): lax.all_to_all(jnp.broadcast_to(own[None], (16,) + own.shape), 'tm', 0, 0...]
    all_gather x1 -> x0, waiting for transfers between devices: 39.5 us -> none  [on_device(): full_sorted = lax.all_gather(sorted_slab, 'orb', axis=3, tiled=True)]
    all_gather x1 -> x0, blocking collectives: 28.1 us -> none  [on_device(): collision = lax.all_gather(summed_rows, 'orb', axis=1, tiled=True)]
    pallas_call x0 -> x2, Pallas kernels: none -> 28.1 us  [the longest x1 23.8 us: on_device(): pl.pallas_call(collide, out_shape=shape((8, 2, 16, N), f32), in_specs=[sm...]
    dynamic_slice x30 -> x1, local copies, waits for them, and re-layouts: 21.2 us -> 0.01 us  [on_device(): rows = lax.dynamic_slice_in_dim(lesser_now, start, 16, 1)]
    ppermute x0 -> x2, starting transfers between devices: none -> 8.69 us  [on_device(): moved.append(lax.ppermute(sent, ('tm', 'orb'), pairs))]
  transfers between devices with their start and end apart: 2 -> 5, of which waited for: 2 -> 4; matrix products, arithmetic and copies ran while one was open for 1% -> 0% of each run, Pallas kernels for 0% -> 0%
where the time goes in v1:
time: 75.4 us; the launch traced here: 74.1 us
  Pallas kernels  28.1 us (37%)
  starting transfers between devices  23.8 us (32%)
  waiting for transfers between devices  19.5 us (26%)
  local copies, waits for them, and re-layouts  1.63 us (2%)
    pallas_call x1, Pallas kernels, on_device(): pl.pallas_call(collide, out_shape=shape((8, 2, 16, N), f32), in_specs=[sm...  23.8 us
    ppermute x2, starting transfers between devices, on_device(): moved.append(lax.ppermute(sent, ('tm', 'orb'), pairs))  8.69 us
    all_to_all x1, waiting for transfers between devices, on_device(): lax.all_to_all(jnp.broadcast_to(own[None], (16,) + own.shape), 'tm', 0, 0...  7.4 us
    ppermute x2, waiting for transfers between devices, on_device(): moved.append(lax.ppermute(sent, ('tm', 'orb'), pairs))  7.03 us
    all_to_all x1, starting transfers between devices, on_device(): brecv = lax.all_to_all(bsend, 'orb', 0, 0, tiled=True)  6.81 us
    all_to_all x1, waiting for transfers between devices, on_device(): own = lax.all_to_all(part, 'orb', 0, 0, tiled=True).sum(0)  5.08 us
    all_to_all x1, starting transfers between devices, on_device(): own = lax.all_to_all(part, 'orb', 0, 0, tiled=True).sum(0)  4.42 us
    pallas_call x1, Pallas kernels, on_device(): pl.pallas_call(pack, out_shape=(shape((8, 2, 2, 4, 16, N), bf), shape((2,...  4.25 us
  transfers between devices with their start and end apart: 5, of which 4 were waited for; matrix products, arithmetic and copies ran while one was open for 0% of the time, Pallas kernels for 0%

profile of v1, /device:TPU:1, one launch (start us, length us, event | category | flops | bytes accessed | tf_op | source)
XLA Modules:
  0.0 74.1 jit_solution(1290835815941821488)
XLA Ops:
  0.0 0.0 copy-start
  0.0 0.0 copy-start.4
  0.0 4.3 %shard_map.73 = (bf16[8,2,2,4,16,128]{5,4,3,2,1,0:T(8,128)(2,1)}, bf16[2,2,2,128,128]{4,3,2,1,0:T(8,128)(2,1)}, bf16[2,2,2,128,128]{4,3,2,1,0:T(8,128)(2,1)}, f32[4]{0:T(128)}) custom-call(s32[512]{0:T(512)} %times.1, bf16[2,2,32,128,128]{4,3,2,1,0:T(8,128)(2,1)} %fwd.1, bf16[2,2,32,16,128]{4,3,2,1,0:T(8,128)(2,1)} %slab.1), custom_call_target="tpu_custom_call" | custom-call | tf_op jit(solution)/shard_map/pallas_call | solution.py:221
  4.3 6.8 %all-to-all-start = ((bf16[8,2,2,4,16,128]{5,4,3,2,1,0:T(8,128)(2,1)}), bf16[8,2,2,4,16,128]{5,4,3,2,1,0:T(8,128)(2,1)S(1)}, u32[]{:S(2)}, u32[]{:S(2)}) async-start(bf16[8,2,2,4,16,128]{5,4,3,2,1,0:T(8,128)(2,1)} %get-tuple-element.12), calls=%async_computation | async-start | bytes 1048576 | tf_op jit(solution)/shard_map/all_to_all | solution.py:238
  11.1 7.3 %collective-permute-start = (bf16[2,2,2,128,128]{4,3,2,1,0:T(8,128)(2,1)}, bf16[2,2,2,128,128]{4,3,2,1,0:T(8,128)(2,1)S(1)}, u32[]{:S(2)}, u32[]{:S(2)}) collective-permute-start(bf16[2,2,2,128,128]{4,3,2,1,0:T(8,128)(2,1)} %get-tuple-element.10), channel_id=1, source_target_pairs={{0,0},{1,81},{2,10},{3,91},{4,20},{5,69},{6,30},{7,79},{8,8},{9,89... | collective-permute-start | bytes 786440 | tf_op jit(solution)/shard_map/ppermute | solution.py:237
  18.4 1.4 %collective-permute-start.1 = (bf16[2,2,2,128,128]{4,3,2,1,0:T(8,128)(2,1)}, bf16[2,2,2,128,128]{4,3,2,1,0:T(8,128)(2,1)S(1)}, u32[]{:S(2)}, u32[]{:S(2)}) collective-permute-start(bf16[2,2,2,128,128]{4,3,2,1,0:T(8,128)(2,1)} %get-tuple-element.11), channel_id=1, source_target_pairs={{0,40},{1,121},{2,50},{3,99},{4,60},{5,109},{6,38},{7,119},{8,48},... | collective-permute-start | bytes 786440 | tf_op jit(solution)/shard_map/ppermute | solution.py:237
  19.8 0.0 copy-done.4
  19.8 4.9 %collective-permute-done.f0 = bf16[2,2,2,128,128]{4,3,2,1,0:T(8,128)(2,1)S(1)} collective-permute-done((bf16[2,2,2,128,128]{4,3,2,1,0:T(8,128)(2,1)}, bf16[2,2,2,128,128]{4,3,2,1,0:T(8,128)(2,1)S(1)}, u32[]{:S(2)}, u32[]{:S(2)}) %collective-permute-start) | collective-permute-done | bytes 262176 | tf_op jit(solution)/shard_map/ppermute | solution.py:237
  24.7 0.0 copy-start.2
  24.7 2.1 %collective-permute-done.1.f1 = bf16[2,2,2,128,128]{4,3,2,1,0:T(8,128)(2,1)S(1)} collective-permute-done((bf16[2,2,2,128,128]{4,3,2,1,0:T(8,128)(2,1)}, bf16[2,2,2,128,128]{4,3,2,1,0:T(8,128)(2,1)S(1)}, u32[]{:S(2)}, u32[]{:S(2)}) %collective-permute-start.1) | collective-permute-done | bytes 262176 | tf_op jit(solution)/shard_map/ppermute | solution.py:237
  26.8 0.0 all-to-all-done.brecv
  26.8 0.0 copy-done.2
  26.8 0.7 copy-done.3
  27.5 0.2 copy-done.1
  27.7 23.8 %shard_map.74 = f32[8,2,16,128]{3,2,1,0:T(8,128)} custom-call(f32[4]{0:T(128)} %get-tuple-element.9.wts, bf16[2,2,2,128,128]{4,3,2,1,0:T(8,128)(2,1)} %copy-done.2, bf16[2,2,2,128,128]{4,3,2,1,0:T(8,128)(2,1)} %copy-done.3, bf16[8,2,2,4,16,128]{5,4,3,2,1,0:T(8,128)(2,1)} %copy-done.1, f32[128,128]{1,0:T(8,128)} %coup.1, s32[128,128]{1,0:T(8,128)} %patt.1), custom_call_target="tpu_custom_call" | custom-call | tf_op jit(solution)/shard_map/pallas_call | solution.py:240
  51.5 4.4 %all-to-all-start.1 = ((f32[8,2,16,128]{3,2,1,0:T(8,128)}), f32[8,2,16,128]{3,2,1,0:T(8,128)S(1)}, u32[]{:S(2)}, u32[]{:S(2)}) async-start(f32[8,2,16,128]{3,2,1,0:T(8,128)} %shard_map.74), calls=%async_computation.1 | async-start | bytes 262144 | tf_op jit(solution)/shard_map/all_to_all | solution.py:248
  56.0 0.0 copy-done
  56.0 0.2 fusion.12
  56.1 5.1 %all-to-all-done.1 = f32[8,2,16,128]{3,2,1,0:T(8,128)S(1)} async-done(((f32[8,2,16,128]{3,2,1,0:T(8,128)}), f32[8,2,16,128]{3,2,1,0:T(8,128)S(1)}, u32[]{:S(2)}, u32[]{:S(2)}) %all-to-all-start.1) | async-done | bytes 131104 | tf_op jit(solution)/shard_map/all_to_all | solution.py:248
  61.2 0.7 broadcast_in_dim.2
  61.9 3.9 %all-to-all-start.2 = ((f32[16,2,16,128]{3,2,1,0:T(8,128)}), f32[16,2,16,128]{3,2,1,0:T(8,128)S(1)}, u32[]{:S(2)}, u32[]{:S(2)}) async-start(f32[16,2,16,128]{3,2,1,0:T(8,128)} %broadcast_in_dim.2), calls=%async_computation.2 | async-start | bytes 524288 | tf_op jit(solution)/shard_map/all_to_all | solution.py:249
  65.9 0.2 fusion
  66.0 7.4 %all-to-all-done.2 = f32[16,2,16,128]{3,2,1,0:T(8,128)S(1)} async-done(((f32[16,2,16,128]{3,2,1,0:T(8,128)}), f32[16,2,16,128]{3,2,1,0:T(8,128)S(1)}, u32[]{:S(2)}, u32[]{:S(2)}) %all-to-all-start.2) | async-done | bytes 262176 | tf_op jit(solution)/shard_map/all_to_all | solution.py:249
  73.5 0.6 fusion.5
  (7 shorter events, 0.1 us)
Async XLA Ops:
  0.0 56.0 %copy-start = (f32[128,128]{1,0:T(8,128)S(1)}, f32[128,128]{1,0:T(8,128)}, u32[]{:S(2)}) copy-start(f32[128,128]{1,0:T(8,128)} %param.12) | copy-start | bytes 196612
  0.0 19.8 %copy-start.4 = (f32[2,128,128]{2,1,0:T(8,128)S(1)}, f32[2,128,128]{2,1,0:T(8,128)}, u32[]{:S(2)}) copy-start(f32[2,128,128]{2,1,0:T(8,128)} %param.13) | copy-start | bytes 393220
  4.3 22.6 %all-to-all-start = ((bf16[8,2,2,4,16,128]{5,4,3,2,1,0:T(8,128)(2,1)}), bf16[8,2,2,4,16,128]{5,4,3,2,1,0:T(8,128)(2,1)S(1)}, u32[]{:S(2)}, u32[]{:S(2)}) async-start(bf16[8,2,2,4,16,128]{5,4,3,2,1,0:T(8,128)(2,1)} %get-tuple-element.12), calls=%async_computation | async-start | bytes 1048576 | tf_op jit(solution)/shard_map/all_to_all | solution.py:238
  11.1 13.6 %collective-permute-start = (bf16[2,2,2,128,128]{4,3,2,1,0:T(8,128)(2,1)}, bf16[2,2,2,128,128]{4,3,2,1,0:T(8,128)(2,1)S(1)}, u32[]{:S(2)}, u32[]{:S(2)}) collective-permute-start(bf16[2,2,2,128,128]{4,3,2,1,0:T(8,128)(2,1)} %get-tuple-element.10), channel_id=1, source_target_pairs={{0,0},{1,81},{2,10},{3,91},{4,20},{5,69},{6,30},{7,79},{8,8},{9,89... | collective-permute-start | bytes 786440 | tf_op jit(solution)/shard_map/ppermute | solution.py:237
  18.4 8.5 %collective-permute-start.1 = (bf16[2,2,2,128,128]{4,3,2,1,0:T(8,128)(2,1)}, bf16[2,2,2,128,128]{4,3,2,1,0:T(8,128)(2,1)S(1)}, u32[]{:S(2)}, u32[]{:S(2)}) collective-permute-start(bf16[2,2,2,128,128]{4,3,2,1,0:T(8,128)(2,1)} %get-tuple-element.11), channel_id=1, source_target_pairs={{0,40},{1,121},{2,50},{3,99},{4,60},{5,109},{6,38},{7,119},{8,48},... | collective-permute-start | bytes 786440 | tf_op jit(solution)/shard_map/ppermute | solution.py:237
  24.7 2.1 %copy-start.2 = (bf16[2,2,2,128,128]{4,3,2,1,0:T(8,128)(2,1)}, bf16[2,2,2,128,128]{4,3,2,1,0:T(8,128)(2,1)S(1)}, u32[]{:S(2)}) copy-start(bf16[2,2,2,128,128]{4,3,2,1,0:T(8,128)(2,1)S(1)} %collective-permute-done.f0) | copy-start | bytes 786436
  26.8 0.7 copy-start.3
  26.8 0.9 %copy-start.1 = (bf16[8,2,2,4,16,128]{5,4,3,2,1,0:T(8,128)(2,1)}, bf16[8,2,2,4,16,128]{5,4,3,2,1,0:T(8,128)(2,1)S(1)}, u32[]{:S(2)}) copy-start(bf16[8,2,2,4,16,128]{5,4,3,2,1,0:T(8,128)(2,1)S(1)} %all-to-all-done.brecv) | copy-start | bytes 1572868
  51.5 9.7 %all-to-all-start.1 = ((f32[8,2,16,128]{3,2,1,0:T(8,128)}), f32[8,2,16,128]{3,2,1,0:T(8,128)S(1)}, u32[]{:S(2)}, u32[]{:S(2)}) async-start(f32[8,2,16,128]{3,2,1,0:T(8,128)} %shard_map.74), calls=%async_computation.1 | async-start | bytes 262144 | tf_op jit(solution)/shard_map/all_to_all | solution.py:248
  61.9 11.5 %all-to-all-start.2 = ((f32[16,2,16,128]{3,2,1,0:T(8,128)}), f32[16,2,16,128]{3,2,1,0:T(8,128)S(1)}, u32[]{:S(2)}, u32[]{:S(2)}) async-start(f32[16,2,16,128]{3,2,1,0:T(8,128)} %broadcast_in_dim.2), calls=%async_computation.2 | async-start | bytes 524288 | tf_op jit(solution)/shard_map/all_to_all | solution.py:249

commit v2 on v1

--- a/solution.py
+++ b/solution.py
@@ -4,6 +4,7 @@
 from jax.experimental import pallas as pl
 from jax.experimental.pallas import tpu as pltpu
 from jax.sharding import PartitionSpec as P
+
 
 N = 128
 bf = jnp.bfloat16
@@ -160,56 +161,51 @@
 
 
 def shift(orb, half):
-    down = 2 * (orb % 2) + half
-    return down, (down + orb // 2) % 4
-
-
-def pack(times, fwd, slab, bsend, f0, f1, wts, seen, sems):
+    down = 2 * (orb & 1) + half
+    return down, (down + (orb >> 1)) & 3
+
+
+def pack(times, fwd, slab, bsend, f0, f1, wts, here, seen, sems):
     me = lax.axis_index("tm")
     orb = lax.axis_index("orb")
-    down = me // 4
-    right = me % 4
+    down = me >> 2
+    right = me & 3
+    rows_in = pltpu.make_async_copy(slab, here, sems.at[4])
+    rows_in.start()
     copies = []
     for half, dst in enumerate((f0, f1)):
         dy, dx = shift(orb, half)
-        row = (((down + dy) % 4) * 4 + (right + dx) % 4) * 32
-
-        def send(slot, found, dst=dst, half=half, row=row):
+        row = ((((down + dy) & 3) << 2) + ((right + dx) & 3)) << 5
+        early = jnp.int32(1 << 20)
+        late = jnp.int32(-1)
+        for slot in range(32):
             when = times[row + slot]
-            mine = when // 32 == me
-
-            @pl.when(mine)
-            def _():
-                pltpu.make_async_copy(fwd.at[:, :, when % 32], dst.at[found], sems.at[2 * half + found]).start()
-
-            return found + mine.astype(jnp.int32)
-
-        lax.fori_loop(0, 32, send, 0)
-        copies += [pltpu.make_async_copy(fwd.at[:, :, 0], dst.at[r], sems.at[2 * half + r]) for r in range(2)]
+            mine = (when >> 5) == me
+            key = slot * 512 + when
+            early = jnp.minimum(early, jnp.where(mine, key, 1 << 20))
+            late = jnp.maximum(late, jnp.where(mine, key, -1))
+        for r, key in enumerate((early, late)):
+            copy = pltpu.make_async_copy(fwd.at[:, :, key & 31], dst.at[r], sems.at[2 * half + r])
+            copy.start()
+            copies.append(copy)
     for e in range(16):
         seen[e] = 0
-
-    def place(slot, carry):
-        when = times[me * 32 + slot]
-        holder = when // 32
+    rows_in.wait()
+    for slot in range(32):
+        when = times[(me << 5) + slot]
+        holder = when >> 5
         rank = seen[holder]
         seen[holder] = rank + 1
-        dy = (down - holder // 4 + 4) % 4
-        dx = (right - holder % 4 + 4) % 4
-        to = ((dx - dy + 4) % 4) * 2 + dy // 2
-        spot = (dy % 2) * 2 + rank
+        dy = (down - (holder >> 2)) & 3
+        dx = (right - (holder & 3)) & 3
+        to = (((dx - dy) & 3) << 1) + (dy >> 1)
+        spot = ((dy & 1) << 1) + rank
         for a in range(2):
             for c in range(2):
-                bsend[to, a, c, spot] = slab[a, c, slot]
-
-        @pl.when(to == orb)
-        def _():
-            edge = jnp.logical_or(when == 0, when == 511)
-            wts[spot] = jnp.where(edge, jnp.float32(0.5), jnp.float32(1.0)) * jnp.float32(HISTORY_STEP)
-
-        return carry
-
-    lax.fori_loop(0, 32, place, 0)
+                bsend[to, a, c, spot] = here[a, c, slot]
+        edge = jnp.logical_or(when == 0, when == 511)
+        weight = jnp.where(edge, jnp.float32(0.5), jnp.float32(1.0)) * jnp.float32(HISTORY_STEP)
+        wts[jnp.where(to == orb, spot, 4)] = weight
     for copy in copies:
         copy.wait()
 
@@ -217,14 +213,17 @@
 def on_device(forward, backward_slab, slot_time, pattern, coupling, hamiltonian, lesser_now):
     smem = pl.BlockSpec(memory_space=pltpu.SMEM)
     vmem = pl.BlockSpec(memory_space=pltpu.VMEM)
+    hbm = pl.BlockSpec(memory_space=pl.ANY)
     shape = jax.ShapeDtypeStruct
     bsend, f0, f1, wts = pl.pallas_call(
         pack,
         out_shape=(shape((8, 2, 2, 4, 16, N), bf), shape((2, 2, 2, N, N), bf), shape((2, 2, 2, N, N), bf),
-                   shape((4,), f32)),
-        in_specs=[smem, pl.BlockSpec(memory_space=pl.ANY), vmem],
+                   shape((8,), f32)),
+        in_specs=[smem, hbm, hbm],
         out_specs=(vmem, vmem, vmem, smem),
-        scratch_shapes=[pltpu.SMEM((16,), jnp.int32), pltpu.SemaphoreType.DMA((4,))],
+        scratch_shapes=[pltpu.VMEM((2, 2, 32, 16, N), bf), pltpu.SMEM((16,), jnp.int32),
+                        pltpu.SemaphoreType.DMA((5,))],
+        compiler_params=pltpu.CompilerParams(vmem_limit_bytes=61 << 20),
     )(slot_time, forward, backward_slab)
     moved = []
     for half, sent in enumerate((f0, f1)):
@@ -244,6 +243,7 @@
         out_specs=vmem,
         scratch_shapes=[V((N, N, N), f32), V((N, N), f32), V((8, 2, N, N), f32), V((8, 2, N, N), f32),
                         V((8, N, 2 * N), f32), V((8, N, 2 * N), bf)],
+        compiler_params=pltpu.CompilerParams(vmem_limit_bytes=24 << 20),
     )(wts, moved[0], moved[1], brecv, coupling, pattern)
     own = lax.all_to_all(part, "orb", 0, 0, tiled=True).sum(0)
     spread = lax.all_to_all(jnp.broadcast_to(own[None], (16,) + own.shape), "tm", 0, 0, tiled=True)
@@ -269,5 +269,4 @@
         P(),
         P(),
     )
-    run = jax.shard_map(on_device, mesh=mesh, in_specs=in_specs, out_specs=P(None, "orb", None), check_vma=False)
-    return run
+    return jax.shard_map(on_device, mesh=mesh, in_specs=in_specs, out_specs=P(None, "orb", None), check_vma=False)

time: 75.4 us -> 73.5 us (0.975)
  Pallas kernels: 28.1 us -> 26.4 us
    pallas_call x1, Pallas kernels: 4.25 us -> 3.25 us  [on_device(): pl.pallas_call(pack, out_shape=(shape((8, 2, 2, 4, 16, N), bf), shape((2,...]
where the time goes in v2:
time: 73.5 us; the launch traced here: 72.2 us
  Pallas kernels  26.4 us (36%)
  starting transfers between devices  23.8 us (32%)
  waiting for transfers between devices  19.5 us (27%)
  local copies, waits for them, and re-layouts  1.42 us (2%)
    pallas_call x1, Pallas kernels, on_device(): pl.pallas_call(collide, out_shape=shape((8, 2, 16, N), f32), in_specs=[sm...  23.1 us
    ppermute x2, starting transfers between devices, on_device(): moved.append(lax.ppermute(sent, ('tm', 'orb'), pairs))  8.69 us
    all_to_all x1, waiting for transfers between devices, on_device(): lax.all_to_all(jnp.broadcast_to(own[None], (16,) + own.shape), 'tm', 0, 0...  7.4 us
    ppermute x2, waiting for transfers between devices, on_device(): moved.append(lax.ppermute(sent, ('tm', 'orb'), pairs))  7.03 us
    all_to_all x1, starting transfers between devices, on_device(): brecv = lax.all_to_all(bsend, 'orb', 0, 0, tiled=True)  6.81 us
    all_to_all x1, waiting for transfers between devices, on_device(): own = lax.all_to_all(part, 'orb', 0, 0, tiled=True).sum(0)  5.08 us
    all_to_all x1, starting transfers between devices, on_device(): own = lax.all_to_all(part, 'orb', 0, 0, tiled=True).sum(0)  4.42 us
    all_to_all x1, starting transfers between devices, on_device(): lax.all_to_all(jnp.broadcast_to(own[None], (16,) + own.shape), 'tm', 0, 0...  3.9 us
  transfers between devices with their start and end apart: 5, of which 4 were waited for; matrix products, arithmetic and copies ran while one was open for 0% of the time, Pallas kernels for 0%

profile of v2, /device:TPU:1, one launch (start us, length us, event | category | flops | bytes accessed | tf_op | source)
XLA Modules:
  0.0 72.2 jit_solution(17562192401573648111)
XLA Ops:
  0.0 0.0 copy-start
  0.0 0.0 copy-start.2
  0.0 3.2 %shard_map.73 = (bf16[8,2,2,4,16,128]{5,4,3,2,1,0:T(8,128)(2,1)}, bf16[2,2,2,128,128]{4,3,2,1,0:T(8,128)(2,1)}, bf16[2,2,2,128,128]{4,3,2,1,0:T(8,128)(2,1)}, f32[8]{0:T(128)}) custom-call(s32[512]{0:T(512)} %times.1, bf16[2,2,32,128,128]{4,3,2,1,0:T(8,128)(2,1)} %fwd.1, bf16[2,2,32,16,128]{4,3,2,1,0:T(8,128)(2,1)} %slab.1), custom_call_target="tpu_custom_call" | custom-call | tf_op jit(solution)/shard_map/pallas_call | solution.py:218
  3.3 6.8 %all-to-all-start = ((bf16[8,2,2,4,16,128]{5,4,3,2,1,0:T(8,128)(2,1)}), bf16[8,2,2,4,16,128]{5,4,3,2,1,0:T(8,128)(2,1)S(1)}, u32[]{:S(2)}, u32[]{:S(2)}) async-start(bf16[8,2,2,4,16,128]{5,4,3,2,1,0:T(8,128)(2,1)} %get-tuple-element.12), calls=%async_computation | async-start | bytes 1048576 | tf_op jit(solution)/shard_map/all_to_all | solution.py:237
  10.1 7.3 %collective-permute-start = (bf16[2,2,2,128,128]{4,3,2,1,0:T(8,128)(2,1)}, bf16[2,2,2,128,128]{4,3,2,1,0:T(8,128)(2,1)S(1)}, u32[]{:S(2)}, u32[]{:S(2)}) collective-permute-start(bf16[2,2,2,128,128]{4,3,2,1,0:T(8,128)(2,1)} %get-tuple-element.10), channel_id=1, source_target_pairs={{0,0},{1,81},{2,10},{3,91},{4,20},{5,69},{6,30},{7,79},{8,8},{9,89... | collective-permute-start | bytes 786440 | tf_op jit(solution)/shard_map/ppermute | solution.py:236
  17.4 1.4 %collective-permute-start.1 = (bf16[2,2,2,128,128]{4,3,2,1,0:T(8,128)(2,1)}, bf16[2,2,2,128,128]{4,3,2,1,0:T(8,128)(2,1)S(1)}, u32[]{:S(2)}, u32[]{:S(2)}) collective-permute-start(bf16[2,2,2,128,128]{4,3,2,1,0:T(8,128)(2,1)} %get-tuple-element.11), channel_id=1, source_target_pairs={{0,40},{1,121},{2,50},{3,99},{4,60},{5,109},{6,38},{7,119},{8,48},... | collective-permute-start | bytes 786440 | tf_op jit(solution)/shard_map/ppermute | solution.py:236
  18.8 0.0 copy-done.4
  18.8 4.9 %collective-permute-done.f0 = bf16[2,2,2,128,128]{4,3,2,1,0:T(8,128)(2,1)S(1)} collective-permute-done((bf16[2,2,2,128,128]{4,3,2,1,0:T(8,128)(2,1)}, bf16[2,2,2,128,128]{4,3,2,1,0:T(8,128)(2,1)S(1)}, u32[]{:S(2)}, u32[]{:S(2)}) %collective-permute-start) | collective-permute-done | bytes 262176 | tf_op jit(solution)/shard_map/ppermute | solution.py:236
  23.7 2.1 %collective-permute-done.1.f1 = bf16[2,2,2,128,128]{4,3,2,1,0:T(8,128)(2,1)S(1)} collective-permute-done((bf16[2,2,2,128,128]{4,3,2,1,0:T(8,128)(2,1)}, bf16[2,2,2,128,128]{4,3,2,1,0:T(8,128)(2,1)S(1)}, u32[]{:S(2)}, u32[]{:S(2)}) %collective-permute-start.1) | collective-permute-done | bytes 262176 | tf_op jit(solution)/shard_map/ppermute | solution.py:236
  25.8 0.0 all-to-all-done.brecv
  25.8 0.0 copy-done.1
  25.8 0.0 copy-done.2
  25.8 0.0 copy-start.3
  25.9 0.6 copy-done.3
  26.5 23.1 %shard_map.74 = f32[8,2,16,128]{3,2,1,0:T(8,128)} custom-call(f32[8]{0:T(128)S(1)} %copy-done.3, bf16[2,2,2,128,128]{4,3,2,1,0:T(8,128)(2,1)S(1)} %collective-permute-done.f0, bf16[2,2,2,128,128]{4,3,2,1,0:T(8,128)(2,1)S(1)} %collective-permute-done.1.f1, bf16[8,2,2,4,16,128]{5,4,3,2,1,0:T(8,128)(2,1)S(1)} %all-to-all-done.brecv, f32[128,128]{1,0:T(8,128)S(1)} %copy-done.1, ...), custom_call_target="tpu_custom_call" | custom-call | tf_op jit(solution)/shard_map/pallas_call | solution.py:239
  49.6 4.4 %all-to-all-start.1 = ((f32[8,2,16,128]{3,2,1,0:T(8,128)}), f32[8,2,16,128]{3,2,1,0:T(8,128)S(1)}, u32[]{:S(2)}, u32[]{:S(2)}) async-start(f32[8,2,16,128]{3,2,1,0:T(8,128)} %shard_map.74), calls=%async_computation.1 | async-start | bytes 262144 | tf_op jit(solution)/shard_map/all_to_all | solution.py:248
  54.0 0.0 copy-done
  54.0 0.2 fusion.12
  54.2 5.1 %all-to-all-done.1 = f32[8,2,16,128]{3,2,1,0:T(8,128)S(1)} async-done(((f32[8,2,16,128]{3,2,1,0:T(8,128)}), f32[8,2,16,128]{3,2,1,0:T(8,128)S(1)}, u32[]{:S(2)}, u32[]{:S(2)}) %all-to-all-start.1) | async-done | bytes 131104 | tf_op jit(solution)/shard_map/all_to_all | solution.py:248
  59.3 0.7 %broadcast_in_dim.2 = f32[16,2,16,128]{3,2,1,0:T(8,128)} broadcast(f32[2,16,128]{2,1,0:T(8,128)S(1)} %reduce_sum.18), dimensions={1,2,3} | broadcast | bytes 278528 | tf_op jit(solution)/shard_map/broadcast_in_dim | solution.py:249
  60.0 3.9 %all-to-all-start.2 = ((f32[16,2,16,128]{3,2,1,0:T(8,128)}), f32[16,2,16,128]{3,2,1,0:T(8,128)S(1)}, u32[]{:S(2)}, u32[]{:S(2)}) async-start(f32[16,2,16,128]{3,2,1,0:T(8,128)} %broadcast_in_dim.2), calls=%async_computation.2 | async-start | bytes 524288 | tf_op jit(solution)/shard_map/all_to_all | solution.py:249
  63.9 0.2 fusion
  64.1 7.4 %all-to-all-done.2 = f32[16,2,16,128]{3,2,1,0:T(8,128)S(1)} async-done(((f32[16,2,16,128]{3,2,1,0:T(8,128)}), f32[16,2,16,128]{3,2,1,0:T(8,128)S(1)}, u32[]{:S(2)}, u32[]{:S(2)}) %all-to-all-start.2) | async-done | bytes 262176 | tf_op jit(solution)/shard_map/all_to_all | solution.py:249
  71.5 0.6 fusion.5
  (7 shorter events, 0.1 us)
Async XLA Ops:
  0.0 54.0 %copy-start = (f32[128,128]{1,0:T(8,128)S(1)}, f32[128,128]{1,0:T(8,128)}, u32[]{:S(2)}) copy-start(f32[128,128]{1,0:T(8,128)} %param.12) | copy-start | bytes 196612
  0.0 18.8 %copy-start.4 = (f32[2,128,128]{2,1,0:T(8,128)S(1)}, f32[2,128,128]{2,1,0:T(8,128)}, u32[]{:S(2)}) copy-start(f32[2,128,128]{2,1,0:T(8,128)} %param.13) | copy-start | bytes 393220
  0.0 25.8 %copy-start.1 = (f32[128,128]{1,0:T(8,128)S(1)}, f32[128,128]{1,0:T(8,128)}, u32[]{:S(2)}) copy-start(f32[128,128]{1,0:T(8,128)} %coup.1) | copy-start | bytes 196612
  0.0 25.8 %copy-start.2 = (s32[128,128]{1,0:T(8,128)S(1)}, s32[128,128]{1,0:T(8,128)}, u32[]{:S(2)}) copy-start(s32[128,128]{1,0:T(8,128)} %patt.1) | copy-start | bytes 196612
  3.3 22.6 %all-to-all-start = ((bf16[8,2,2,4,16,128]{5,4,3,2,1,0:T(8,128)(2,1)}), bf16[8,2,2,4,16,128]{5,4,3,2,1,0:T(8,128)(2,1)S(1)}, u32[]{:S(2)}, u32[]{:S(2)}) async-start(bf16[8,2,2,4,16,128]{5,4,3,2,1,0:T(8,128)(2,1)} %get-tuple-element.12), calls=%async_computation | async-start | bytes 1048576 | tf_op jit(solution)/shard_map/all_to_all | solution.py:237
  10.1 13.6 %collective-permute-start = (bf16[2,2,2,128,128]{4,3,2,1,0:T(8,128)(2,1)}, bf16[2,2,2,128,128]{4,3,2,1,0:T(8,128)(2,1)S(1)}, u32[]{:S(2)}, u32[]{:S(2)}) collective-permute-start(bf16[2,2,2,128,128]{4,3,2,1,0:T(8,128)(2,1)} %get-tuple-element.10), channel_id=1, source_target_pairs={{0,0},{1,81},{2,10},{3,91},{4,20},{5,69},{6,30},{7,79},{8,8},{9,89... | collective-permute-start | bytes 786440 | tf_op jit(solution)/shard_map/ppermute | solution.py:236
  17.4 8.5 %collective-permute-start.1 = (bf16[2,2,2,128,128]{4,3,2,1,0:T(8,128)(2,1)}, bf16[2,2,2,128,128]{4,3,2,1,0:T(8,128)(2,1)S(1)}, u32[]{:S(2)}, u32[]{:S(2)}) collective-permute-start(bf16[2,2,2,128,128]{4,3,2,1,0:T(8,128)(2,1)} %get-tuple-element.11), channel_id=1, source_target_pairs={{0,40},{1,121},{2,50},{3,99},{4,60},{5,109},{6,38},{7,119},{8,48},... | collective-permute-start | bytes 786440 | tf_op jit(solution)/shard_map/ppermute | solution.py:236
  25.8 0.7 copy-start.3
  49.6 9.7 %all-to-all-start.1 = ((f32[8,2,16,128]{3,2,1,0:T(8,128)}), f32[8,2,16,128]{3,2,1,0:T(8,128)S(1)}, u32[]{:S(2)}, u32[]{:S(2)}) async-start(f32[8,2,16,128]{3,2,1,0:T(8,128)} %shard_map.74), calls=%async_computation.1 | async-start | bytes 262144 | tf_op jit(solution)/shard_map/all_to_all | solution.py:248
  60.0 11.5 %all-to-all-start.2 = ((f32[16,2,16,128]{3,2,1,0:T(8,128)}), f32[16,2,16,128]{3,2,1,0:T(8,128)S(1)}, u32[]{:S(2)}, u32[]{:S(2)}) async-start(f32[16,2,16,128]{3,2,1,0:T(8,128)} %broadcast_in_dim.2), calls=%async_computation.2 | async-start | bytes 524288 | tf_op jit(solution)/shard_map/all_to_all | solution.py:249

commit v3 on v2

--- a/solution.py
+++ b/solution.py
@@ -11,6 +11,7 @@
 f32 = jnp.float32
 HISTORY_STEP = 0.02
 UPDATE_STEP = 0.5
+STEPS = N // 8
 UNITS = [(kk, a) for kk in range(4) for a in range(2)]
 
 
@@ -26,12 +27,27 @@
     return jnp.concatenate(parts, axis=1)
 
 
-def collide(wts, f0, f1, brecv, coup, patt, out, vb, vv, ft, bt, dirt, sig):
+def shift(orb, half):
+    down = 2 * (orb & 1) + half
+    return down, (down + (orb >> 1)) & 3
+
+
+def matches(times, row, holder):
+    early = jnp.int32(1 << 20)
+    late = jnp.int32(-1)
+    for slot in range(32):
+        when = times[row + slot]
+        mine = (when >> 5) == holder
+        key = slot * 512 + when
+        early = jnp.minimum(early, jnp.where(mine, key, 1 << 20))
+        late = jnp.maximum(late, jnp.where(mine, key, -1))
+    return early & 511, late & 511
+
+
+def collide(times, f0, f1, brecv, coup, patt, out, vb, vv, ft, bt, dirt, sig):
     masked = coup[...] * patt[...].astype(f32)
     inter = ((masked + masked.T) * 0.5).astype(bf)
     vv[...] = inter.astype(f32)
-    for m in range(N):
-        vb[m] = jnp.broadcast_to(vv[:, m:m + 1], (N, N))
 
     def fmat(kk, a, c):
         return (f0, f1)[kk // 2][kk % 2, a, c]
@@ -79,7 +95,7 @@
             half.append(cat1([cat0([w * fvr for w in v]), cat0([w * fvi for w in v])]))
         return cat0(half)
 
-    def lhs_rows(u, m):
+    def lhs_rows(u, m, first):
         re, im = [], []
         for x in range(2):
             bvr = rows16(bt[u, 0, pl.ds(m + x, 1), :])
@@ -89,7 +105,12 @@
                 sl = slice(16 * i, 16 * i + 16)
                 a = ft[u, 0, sl].astype(bf)
                 b = ft[u, 1, sl].astype(bf)
-                v = vb[m + x, sl].astype(bf)
+                if first:
+                    wide = jnp.broadcast_to(vv[sl, m + x:m + x + 1], (16, N))
+                    vb[m + x, sl] = wide
+                else:
+                    wide = vb[m + x, sl]
+                v = wide.astype(bf)
                 pr.append((a * bvr - b * bvi) * v)
                 pi.append((a * bvi + b * bvr) * v)
             re.append(cat0(pr))
@@ -97,44 +118,52 @@
         return cat1(re), cat1(im)
 
     def exchange(*flat):
-        def acc(u, x, c):
-            return flat[4 * (u % 2) + 2 * x + c]
-
-        def step(u, t, last=False):
+        def step(u, par, t, first=False, last=False):
+            acc = flat[4 * par:4 * par + 4]
             for q in range(2):
                 base = 8 * t + 4 * q
-                lhs = [lhs_rows(u, base + 2 * x) for x in range(2)]
+                lhs = [lhs_rows(u, base + 2 * x, first) for x in range(2)]
                 for x in range(2):
-                    pltpu.matmul_acc_lhs(acc(u, x, 0), lhs[x][0], load_staged_rhs=q)
+                    pltpu.matmul_acc_lhs(acc[2 * x], lhs[x][0], load_staged_rhs=q)
                 if not (last and q):
                     for x in range(2):
                         pltpu.matmul_push_rhs(weights(u, base + 4 + 2 * x), 1 - q, x)
-                elif u < 7:
+                elif not (isinstance(u, int) and u == 7):
                     for x in range(2):
                         pltpu.matmul_push_rhs(weights(u + 1, 2 * x), 0, x)
                 for x in range(2):
-                    pltpu.matmul_acc_lhs(acc(u, x, 1), lhs[x][1])
-
-        def finish(u):
-            rp = pltpu.matmul_pop(acc(u, 0, 0)) + pltpu.matmul_pop(acc(u, 1, 0))
-            rq = pltpu.matmul_pop(acc(u, 0, 1)) + pltpu.matmul_pop(acc(u, 1, 1))
+                    pltpu.matmul_acc_lhs(acc[2 * x + 1], lhs[x][1])
+
+        def finish(u, par):
+            acc = flat[4 * par:4 * par + 4]
+            rp = pltpu.matmul_pop(acc[0]) + pltpu.matmul_pop(acc[2])
+            rq = pltpu.matmul_pop(acc[1]) + pltpu.matmul_pop(acc[3])
             sig[u, :, :N] = (dirt[u, :, :N] - (rp[:, :N] - rq[:, N:])).astype(bf)
             sig[u, :, N:] = (dirt[u, :, N:] - (rp[:, N:] + rq[:, :N])).astype(bf)
 
+        def unit(u, par):
+            step(u, par, 0)
+            finish(u - 1, 1 - par)
+
+            def loop(t, inner):
+                step(u, par, t)
+                return inner
+
+            lax.fori_loop(1, STEPS - 1, loop, 0, unroll=7)
+            step(u, par, STEPS - 1, last=True)
+
+        def pair(p, carry):
+            unit(2 * p + 1, 1)
+            unit(2 * p + 2, 0)
+            return carry
+
         for x in range(2):
             pltpu.matmul_push_rhs(weights(0, 2 * x), 0, x)
-        for u in range(8):
-            step(u, 0)
-            if u:
-                finish(u - 1)
-
-            def loop(t, carry):
-                step(u, t)
-                return carry
-
-            lax.fori_loop(1, N // 8 - 1, loop, 0)
-            step(u, N // 8 - 1, True)
-        finish(7)
+        for t in range(STEPS):
+            step(0, 0, t, first=True, last=t == STEPS - 1)
+        lax.fori_loop(0, 3, pair, 0)
+        unit(7, 1)
+        finish(7, 1)
 
     pl.run_scoped(exchange, *[pltpu.ACC(x)((N, 2 * N), f32) for x in (0, 0, 1, 1, 0, 0, 1, 1)])
 
@@ -146,6 +175,14 @@
                 br, bi = -br, -bi
             pltpu.matmul_push_rhs(cat0([cat1([br, bi]), cat1([-bi, br])]), a, kk % 2)
             pltpu.matmul_acc_lhs(accs[kk], sig[u], load_staged_rhs=a)
+        me = lax.axis_index("tm")
+        wts = []
+        for half in range(2):
+            dy, dx = shift(lax.axis_index("orb"), half)
+            holder = ((((me >> 2) - dy) & 3) << 2) + (((me & 3) - dx) & 3)
+            for when in matches(times, me << 5, holder):
+                edge = jnp.logical_or(when == 0, when == 511)
+                wts.append(jnp.where(edge, jnp.float32(0.5), jnp.float32(1.0)) * jnp.float32(HISTORY_STEP))
         total = wts[0] * pltpu.matmul_pop(accs[0])
         for kk in range(1, 4):
             total += wts[kk] * pltpu.matmul_pop(accs[kk])
@@ -160,12 +197,7 @@
     pl.run_scoped(product, *[pltpu.ACC(kk % 2)((N, 2 * N), f32) for kk in range(4)])
 
 
-def shift(orb, half):
-    down = 2 * (orb & 1) + half
-    return down, (down + (orb >> 1)) & 3
-
-
-def pack(times, fwd, slab, bsend, f0, f1, wts, here, seen, sems):
+def pack(times, fwd, slab, bsend, f0, f1, here, seen, sems):
     me = lax.axis_index("tm")
     orb = lax.axis_index("orb")
     down = me >> 2
@@ -176,16 +208,8 @@
     for half, dst in enumerate((f0, f1)):
         dy, dx = shift(orb, half)
         row = ((((down + dy) & 3) << 2) + ((right + dx) & 3)) << 5
-        early = jnp.int32(1 << 20)
-        late = jnp.int32(-1)
-        for slot in range(32):
-            when = times[row + slot]
-            mine = (when >> 5) == me
-            key = slot * 512 + when
-            early = jnp.minimum(early, jnp.where(mine, key, 1 << 20))
-            late = jnp.maximum(late, jnp.where(mine, key, -1))
-        for r, key in enumerate((early, late)):
-            copy = pltpu.make_async_copy(fwd.at[:, :, key & 31], dst.at[r], sems.at[2 * half + r])
+        for r, when in enumerate(matches(times, row, me)):
+            copy = pltpu.make_async_copy(fwd.at[:, :, when & 31], dst.at[r], sems.at[2 * half + r])
             copy.start()
             copies.append(copy)
     for e in range(16):
@@ -203,9 +227,6 @@
         for a in range(2):
             for c in range(2):
                 bsend[to, a, c, spot] = here[a, c, slot]
-        edge = jnp.logical_or(when == 0, when == 511)
-        weight = jnp.where(edge, jnp.float32(0.5), jnp.float32(1.0)) * jnp.float32(HISTORY_STEP)
-        wts[jnp.where(to == orb, spot, 4)] = weight
     for copy in copies:
         copy.wait()
 
@@ -215,12 +236,11 @@
     vmem = pl.BlockSpec(memory_space=pltpu.VMEM)
     hbm = pl.BlockSpec(memory_space=pl.ANY)
     shape = jax.ShapeDtypeStruct
-    bsend, f0, f1, wts = pl.pallas_call(
+    bsend, f0, f1 = pl.pallas_call(
         pack,
-        out_shape=(shape((8, 2, 2, 4, 16, N), bf), shape((2, 2, 2, N, N), bf), shape((2, 2, 2, N, N), bf),
-                   shape((8,), f32)),
+        out_shape=(shape((8, 2, 2, 4, 16, N), bf), shape((2, 2, 2, N, N), bf), shape((2, 2, 2, N, N), bf)),
         in_specs=[smem, hbm, hbm],
-        out_specs=(vmem, vmem, vmem, smem),
+        out_specs=(vmem, vmem, vmem),
         scratch_shapes=[pltpu.VMEM((2, 2, 32, 16, N), bf), pltpu.SMEM((16,), jnp.int32),
                         pltpu.SemaphoreType.DMA((5,))],
         compiler_params=pltpu.CompilerParams(vmem_limit_bytes=61 << 20),
@@ -244,7 +264,7 @@
         scratch_shapes=[V((N, N, N), f32), V((N, N), f32), V((8, 2, N, N), f32), V((8, 2, N, N), f32),
                         V((8, N, 2 * N), f32), V((8, N, 2 * N), bf)],
         compiler_params=pltpu.CompilerParams(vmem_limit_bytes=24 << 20),
-    )(wts, moved[0], moved[1], brecv, coupling, pattern)
+    )(slot_time, moved[0], moved[1], brecv, coupling, pattern)
     own = lax.all_to_all(part, "orb", 0, 0, tiled=True).sum(0)
     spread = lax.all_to_all(jnp.broadcast_to(own[None], (16,) + own.shape), "tm", 0, 0, tiled=True)
     start = lax.axis_index("orb") * 16

time: 73.5 us -> 72.5 us (0.986)
  no operation moved by 1% of the time
where the time goes in v3:
time: 72.5 us; the launch traced here: 71.2 us
  Pallas kernels  26 us (36%)
  starting transfers between devices  23.8 us (33%)
  waiting for transfers between devices  19.5 us (27%)
  local copies, waits for them, and re-layouts  0.77 us (1%)
    pallas_call x1, Pallas kernels, on_device(): pl.pallas_call(collide, out_shape=shape((8, 2, 16, N), f32), in_specs=[sm...  22.9 us
    ppermute x2, starting transfers between devices, on_device(): moved.append(lax.ppermute(sent, ('tm', 'orb'), pairs))  8.69 us
    all_to_all x1, waiting for transfers between devices, on_device(): lax.all_to_all(jnp.broadcast_to(own[None], (16,) + own.shape), 'tm', 0, 0...  7.4 us
    ppermute x2, waiting for transfers between devices, on_device(): moved.append(lax.ppermute(sent, ('tm', 'orb'), pairs))  7.03 us
    all_to_all x1, starting transfers between devices, on_device(): brecv = lax.all_to_all(bsend, 'orb', 0, 0, tiled=True)  6.81 us
    all_to_all x1, waiting for transfers between devices, on_device(): own = lax.all_to_all(part, 'orb', 0, 0, tiled=True).sum(0)  5.08 us
    all_to_all x1, starting transfers between devices, on_device(): own = lax.all_to_all(part, 'orb', 0, 0, tiled=True).sum(0)  4.41 us
    all_to_all x1, starting transfers between devices, on_device(): lax.all_to_all(jnp.broadcast_to(own[None], (16,) + own.shape), 'tm', 0, 0...  3.91 us
  transfers between devices with their start and end apart: 5, of which 4 were waited for; matrix products, arithmetic and copies ran while one was open for 0% of the time, Pallas kernels for 0%

profile of v3, /device:TPU:1, one launch (start us, length us, event | category | flops | bytes accessed | tf_op | source)
XLA Modules:
  0.0 71.2 jit_solution(3611408866889345719)
XLA Ops:
  0.0 0.0 copy-start
  0.0 0.0 copy-start.1
  0.0 0.0 copy-start.2
  0.0 3.1 %shard_map.73 = (bf16[8,2,2,4,16,128]{5,4,3,2,1,0:T(8,128)(2,1)}, bf16[2,2,2,128,128]{4,3,2,1,0:T(8,128)(2,1)}, bf16[2,2,2,128,128]{4,3,2,1,0:T(8,128)(2,1)}) custom-call(s32[512]{0:T(512)} %times.3, bf16[2,2,32,128,128]{4,3,2,1,0:T(8,128)(2,1)} %fwd.1, bf16[2,2,32,16,128]{4,3,2,1,0:T(8,128)(2,1)} %slab.1), custom_call_target="tpu_custom_call" | custom-call | tf_op jit(solution)/shard_map/pallas_call | solution.py:239
  3.2 6.8 %all-to-all-start = ((bf16[8,2,2,4,16,128]{5,4,3,2,1,0:T(8,128)(2,1)}), bf16[8,2,2,4,16,128]{5,4,3,2,1,0:T(8,128)(2,1)S(1)}, u32[]{:S(2)}, u32[]{:S(2)}) async-start(bf16[8,2,2,4,16,128]{5,4,3,2,1,0:T(8,128)(2,1)} %get-tuple-element.10), calls=%async_computation | async-start | bytes 1048576 | tf_op jit(solution)/shard_map/all_to_all | solution.py:257
  10.0 7.3 %collective-permute-start = (bf16[2,2,2,128,128]{4,3,2,1,0:T(8,128)(2,1)}, bf16[2,2,2,128,128]{4,3,2,1,0:T(8,128)(2,1)S(1)}, u32[]{:S(2)}, u32[]{:S(2)}) collective-permute-start(bf16[2,2,2,128,128]{4,3,2,1,0:T(8,128)(2,1)} %get-tuple-element.8), channel_id=1, source_target_pairs={{0,0},{1,81},{2,10},{3,91},{4,20},{5,69},{6,30},{7,79},{8,8},{9,89... | collective-permute-start | bytes 786440 | tf_op jit(solution)/shard_map/ppermute | solution.py:256
  17.3 1.4 %collective-permute-start.1 = (bf16[2,2,2,128,128]{4,3,2,1,0:T(8,128)(2,1)}, bf16[2,2,2,128,128]{4,3,2,1,0:T(8,128)(2,1)S(1)}, u32[]{:S(2)}, u32[]{:S(2)}) collective-permute-start(bf16[2,2,2,128,128]{4,3,2,1,0:T(8,128)(2,1)} %get-tuple-element.9), channel_id=1, source_target_pairs={{0,40},{1,121},{2,50},{3,99},{4,60},{5,109},{6,38},{7,119},{8,48},... | collective-permute-start | bytes 786440 | tf_op jit(solution)/shard_map/ppermute | solution.py:256
  18.7 0.0 copy-done.4
  18.7 4.9 %collective-permute-done.f0 = bf16[2,2,2,128,128]{4,3,2,1,0:T(8,128)(2,1)S(1)} collective-permute-done((bf16[2,2,2,128,128]{4,3,2,1,0:T(8,128)(2,1)}, bf16[2,2,2,128,128]{4,3,2,1,0:T(8,128)(2,1)S(1)}, u32[]{:S(2)}, u32[]{:S(2)}) %collective-permute-start) | collective-permute-done | bytes 262176 | tf_op jit(solution)/shard_map/ppermute | solution.py:256
  23.6 2.1 %collective-permute-done.1.f1 = bf16[2,2,2,128,128]{4,3,2,1,0:T(8,128)(2,1)S(1)} collective-permute-done((bf16[2,2,2,128,128]{4,3,2,1,0:T(8,128)(2,1)}, bf16[2,2,2,128,128]{4,3,2,1,0:T(8,128)(2,1)S(1)}, u32[]{:S(2)}, u32[]{:S(2)}) %collective-permute-start.1) | collective-permute-done | bytes 262176 | tf_op jit(solution)/shard_map/ppermute | solution.py:256
  25.7 0.0 all-to-all-done.brecv
  25.8 0.0 copy-done.3
  25.8 0.0 copy-done.1
  25.8 0.0 copy-done.2
  25.8 22.9 %shard_map.74 = f32[8,2,16,128]{3,2,1,0:T(8,128)} custom-call(s32[512]{0:T(512)S(1)} %copy-done.3, bf16[2,2,2,128,128]{4,3,2,1,0:T(8,128)(2,1)S(1)} %collective-permute-done.f0, bf16[2,2,2,128,128]{4,3,2,1,0:T(8,128)(2,1)S(1)} %collective-permute-done.1.f1, bf16[8,2,2,4,16,128]{5,4,3,2,1,0:T(8,128)(2,1)S(1)} %all-to-all-done.brecv, ...), custom_call_target="tpu_custom_call" | custom-call | tf_op jit(solution)/shard_map/pallas_call | solution.py:259
  48.6 4.4 %all-to-all-start.1 = ((f32[8,2,16,128]{3,2,1,0:T(8,128)}), f32[8,2,16,128]{3,2,1,0:T(8,128)S(1)}, u32[]{:S(2)}, u32[]{:S(2)}) async-start(f32[8,2,16,128]{3,2,1,0:T(8,128)} %shard_map.74), calls=%async_computation.1 | async-start | bytes 262144 | tf_op jit(solution)/shard_map/all_to_all | solution.py:268
  53.0 0.0 copy-done
  53.0 0.2 fusion.12
  53.2 5.1 %all-to-all-done.1 = f32[8,2,16,128]{3,2,1,0:T(8,128)S(1)} async-done(((f32[8,2,16,128]{3,2,1,0:T(8,128)}), f32[8,2,16,128]{3,2,1,0:T(8,128)S(1)}, u32[]{:S(2)}, u32[]{:S(2)}) %all-to-all-start.1) | async-done | bytes 131104 | tf_op jit(solution)/shard_map/all_to_all | solution.py:268
  58.3 0.7 %broadcast_in_dim.2 = f32[16,2,16,128]{3,2,1,0:T(8,128)} broadcast(f32[2,16,128]{2,1,0:T(8,128)S(1)} %reduce_sum.18), dimensions={1,2,3} | broadcast | bytes 278528 | tf_op jit(solution)/shard_map/broadcast_in_dim | solution.py:269
  59.0 3.9 %all-to-all-start.2 = ((f32[16,2,16,128]{3,2,1,0:T(8,128)}), f32[16,2,16,128]{3,2,1,0:T(8,128)S(1)}, u32[]{:S(2)}, u32[]{:S(2)}) async-start(f32[16,2,16,128]{3,2,1,0:T(8,128)} %broadcast_in_dim.2), calls=%async_computation.2 | async-start | bytes 524288 | tf_op jit(solution)/shard_map/all_to_all | solution.py:269
  63.0 0.2 fusion
  63.1 7.4 %all-to-all-done.2 = f32[16,2,16,128]{3,2,1,0:T(8,128)S(1)} async-done(((f32[16,2,16,128]{3,2,1,0:T(8,128)}), f32[16,2,16,128]{3,2,1,0:T(8,128)S(1)}, u32[]{:S(2)}, u32[]{:S(2)}) %all-to-all-start.2) | async-done | bytes 262176 | tf_op jit(solution)/shard_map/all_to_all | solution.py:269
  70.6 0.6 fusion.5
  (7 shorter events, 0.1 us)
Async XLA Ops:
  0.0 53.0 %copy-start = (f32[128,128]{1,0:T(8,128)S(1)}, f32[128,128]{1,0:T(8,128)}, u32[]{:S(2)}) copy-start(f32[128,128]{1,0:T(8,128)} %param.12) | copy-start | bytes 196612
  0.0 25.7 %copy-start.3 = (s32[512]{0:T(512)S(1)}, s32[512]{0:T(512)}, u32[]{:S(2)}) copy-start(s32[512]{0:T(512)} %times.3) | copy-start | bytes 6148
  0.0 18.7 %copy-start.4 = (f32[2,128,128]{2,1,0:T(8,128)S(1)}, f32[2,128,128]{2,1,0:T(8,128)}, u32[]{:S(2)}) copy-start(f32[2,128,128]{2,1,0:T(8,128)} %param.13) | copy-start | bytes 393220
  0.0 25.7 %copy-start.1 = (f32[128,128]{1,0:T(8,128)S(1)}, f32[128,128]{1,0:T(8,128)}, u32[]{:S(2)}) copy-start(f32[128,128]{1,0:T(8,128)} %coup.1) | copy-start | bytes 196612
  0.0 25.7 %copy-start.2 = (s32[128,128]{1,0:T(8,128)S(1)}, s32[128,128]{1,0:T(8,128)}, u32[]{:S(2)}) copy-start(s32[128,128]{1,0:T(8,128)} %patt.1) | copy-start | bytes 196612
  3.2 22.6 %all-to-all-start = ((bf16[8,2,2,4,16,128]{5,4,3,2,1,0:T(8,128)(2,1)}), bf16[8,2,2,4,16,128]{5,4,3,2,1,0:T(8,128)(2,1)S(1)}, u32[]{:S(2)}, u32[]{:S(2)}) async-start(bf16[8,2,2,4,16,128]{5,4,3,2,1,0:T(8,128)(2,1)} %get-tuple-element.10), calls=%async_computation | async-start | bytes 1048576 | tf_op jit(solution)/shard_map/all_to_all | solution.py:257
  10.0 13.6 %collective-permute-start = (bf16[2,2,2,128,128]{4,3,2,1,0:T(8,128)(2,1)}, bf16[2,2,2,128,128]{4,3,2,1,0:T(8,128)(2,1)S(1)}, u32[]{:S(2)}, u32[]{:S(2)}) collective-permute-start(bf16[2,2,2,128,128]{4,3,2,1,0:T(8,128)(2,1)} %get-tuple-element.8), channel_id=1, source_target_pairs={{0,0},{1,81},{2,10},{3,91},{4,20},{5,69},{6,30},{7,79},{8,8},{9,89... | collective-permute-start | bytes 786440 | tf_op jit(solution)/shard_map/ppermute | solution.py:256
  17.3 8.5 %collective-permute-start.1 = (bf16[2,2,2,128,128]{4,3,2,1,0:T(8,128)(2,1)}, bf16[2,2,2,128,128]{4,3,2,1,0:T(8,128)(2,1)S(1)}, u32[]{:S(2)}, u32[]{:S(2)}) collective-permute-start(bf16[2,2,2,128,128]{4,3,2,1,0:T(8,128)(2,1)} %get-tuple-element.9), channel_id=1, source_target_pairs={{0,40},{1,121},{2,50},{3,99},{4,60},{5,109},{6,38},{7,119},{8,48},... | collective-permute-start | bytes 786440 | tf_op jit(solution)/shard_map/ppermute | solution.py:256
  48.6 9.7 %all-to-all-start.1 = ((f32[8,2,16,128]{3,2,1,0:T(8,128)}), f32[8,2,16,128]{3,2,1,0:T(8,128)S(1)}, u32[]{:S(2)}, u32[]{:S(2)}) async-start(f32[8,2,16,128]{3,2,1,0:T(8,128)} %shard_map.74), calls=%async_computation.1 | async-start | bytes 262144 | tf_op jit(solution)/shard_map/all_to_all | solution.py:268
  59.0 11.5 %all-to-all-start.2 = ((f32[16,2,16,128]{3,2,1,0:T(8,128)}), f32[16,2,16,128]{3,2,1,0:T(8,128)S(1)}, u32[]{:S(2)}, u32[]{:S(2)}) async-start(f32[16,2,16,128]{3,2,1,0:T(8,128)} %broadcast_in_dim.2), calls=%async_computation.2 | async-start | bytes 524288 | tf_op jit(solution)/shard_map/all_to_all | solution.py:269
